TPU v7x, 256 devices: a whole 4x4x8 slice. The times are simulated.
256 devices in a mesh: ha: 16 (over y, x), wa: 16 (over z, core).
Axes of the slice: x: 4, y: 4, z: 8, core: 2. Of those that a mesh axis runs over, the one named last changes fastest.
Arguments:
- latent: bfloat16 [720, 640, 96], P('ha', 'wa'), may hold values from -6 to 6
- frame_cache: bfloat16 [2, 720, 640, 96], P(None, 'ha', 'wa'), may hold values from -6 to 6
- norm_gain: float32 [96], replicated, may hold values from 0.5 to 2
- conv_bias: float32 [96], replicated, may hold values from -3 to 3
- conv_weight: bfloat16 [96, 2592], P('ha', 'wa'), may hold values from -0.125 to 0.125
- grad_out: bfloat16 [720, 640, 96], P('ha', 'wa'), may hold values from -6 to 6
Outputs:
- output: bfloat16 [720, 640, 96], P('ha', 'wa')
- grad_latent: bfloat16 [720, 640, 96], P('ha', 'wa')
- grad_weight: float32 [96, 2592], P('ha', 'wa')
All inputs are finite; a program needn't handle non-finite values.
Results may differ from a plain program's by a relative error of at most 0.0023.
Values may be sent and summed in bfloat16 or wider, within the bound.
A program may use at most 64 MiB of HBM per device.

v0:
```python
import jax
import jax.numpy as jnp
from jax import lax
from jax.sharding import PartitionSpec as P


def padded_2(block, sides, width):
    for axis, dim in sides:
        count = lax.axis_size(axis)
        forward = [(i, i + 1) for i in range(count - 1)]
        backward = [(target, source) for source, target in forward]
        low = lax.ppermute(
            lax.slice_in_dim(block, block.shape[dim] - width, None, axis=dim), axis, forward
        )
        high = lax.ppermute(lax.slice_in_dim(block, 0, width, axis=dim), axis, backward)
        block = jnp.concatenate([low, block, high], axis=dim)
    return block


def activate(values, norm_gain):
    scale = lax.rsqrt(jnp.mean(values * values, axis=-1, keepdims=True) + 1e-06)
    return jax.nn.silu(values * scale * norm_gain)


def local(latent, frame_cache, norm_gain, conv_bias, conv_weight, grad_out):
    height = latent.shape[0]
    width = latent.shape[1]
    channels = latent.shape[2]
    latent_float = latent.astype(jnp.float32)
    activated = activate(latent_float, norm_gain).astype(jnp.bfloat16)
    frames = jnp.concatenate([frame_cache, activated[None]], axis=0)
    padded = padded_2(frames, (("ha", 1), ("wa", 2)), 1)
    weight_part = lax.all_gather(conv_weight, "wa", axis=1, tiled=True)
    full_weight = lax.all_gather(weight_part, "ha", axis=0, tiled=True)
    grad_padded = padded_2(grad_out, (("ha", 0), ("wa", 1)), 1)
    grad_flat = grad_out.reshape(-1, channels)
    total = jnp.zeros((height * width, channels), jnp.float32)
    back_total = jnp.zeros((height * width, channels), jnp.float32)
    pieces = []
    for time_tap in range(3):
        for row_tap in range(3):
            for col_tap in range(3):
                offset = (9 * time_tap + 3 * row_tap + col_tap) * channels
                tap_weight = full_weight[:, offset : offset + channels]
                slab_rows = padded[
                    time_tap, row_tap : row_tap + height, col_tap : col_tap + width
                ].reshape(-1, channels)
                total = total + lax.dot_general(
                    slab_rows,
                    tap_weight,
                    (((1,), (1,)), ((), ())),
                    preferred_element_type=jnp.float32,
                )
                pieces.append(
                    lax.dot_general(
                        grad_flat,
                        slab_rows,
                        (((0,), (0,)), ((), ())),
                        preferred_element_type=jnp.float32,
                    )
                )
                if time_tap == 2:
                    shifted = grad_padded[
                        2 - row_tap : 2 - row_tap + height, 2 - col_tap : 2 - col_tap + width
                    ].reshape(-1, channels)
                    back_total = back_total + jnp.dot(
                        shifted, tap_weight, preferred_element_type=jnp.float32
                    )
    output = (latent_float + conv_bias + total.reshape(height, width, channels)).astype(
        jnp.bfloat16
    )
    weight_term = jnp.concatenate(pieces, axis=1)
    partial_cols = lax.psum_scatter(weight_term, "wa", scatter_dimension=1, tiled=True)
    grad_weight = lax.psum_scatter(partial_cols, "ha", scatter_dimension=0, tiled=True)
    unused, pullback = jax.vjp(lambda values: activate(values, norm_gain), latent_float)
    grad_latent = (
        grad_out.astype(jnp.float32) + pullback(back_total.reshape(height, width, channels))[0]
    ).astype(jnp.bfloat16)
    return (output, grad_latent, grad_weight)


def solution(mesh):
    placed = (
        P("ha", "wa", None),
        P(None, "ha", "wa", None),
        P(),
        P(),
        P("ha", "wa"),
        P("ha", "wa", None),
    )
    return jax.shard_map(
        local,
        mesh=mesh,
        in_specs=placed,
        out_specs=(P("ha", "wa", None), P("ha", "wa", None), P("ha", "wa")),
        check_vma=False,
    )
```

profile of v0, /device:TPU:96, one launch (start us, length us, event | category | flops | bytes accessed | tf_op | source)
XLA Modules:
  0.0 332.5 jit_solution(2743348610710656579)
XLA Ops:
  8.0 3.4 %collective-permute-start.4 = (bf16[1,40,96]{2,1,0:T(8,128)(2,1)S(1)}, bf16[1,40,96]{2,1,0:T(8,128)(2,1)S(1)}, u32[]{:S(2)}, u32[]{:S(2)}) collective-permute-start(bf16[1,40,96]{2,1,0:T(8,128)(2,1)S(1)} %get-tuple-element.54), channel_id=1, source_target_pairs={{0,16},{16,32},{32,48},{48,64},{64,80},{80,96},{96,112},{112,128},... | collective-permute-start | bytes 23048 | tf_op jit(solution)/shard_map/ppermute | solution.py:12
  11.4 1.3 collective-permute-start.5
  12.7 16.4 %all-gather = bf16[16,162,6]{1,2,0:T(8,128)(2,1)S(1)} all-gather(bf16[1,162,6]{1,2,0:T(8,128)(2,1)} %bitcast.289), channel_id=1, replica_groups=mesh['ha'=16,'wa'=16] {'wa'}, dimensions={0}, use_global_device_ids=true | all-gather | bytes 33048 | tf_op jit(solution)/shard_map/all_gather | solution.py:33
  29.2 1.3 fusion.14
  30.6 1.1 slice.251
  32.0 27.5 %all-gather.1 = bf16[16,6,2592]{2,1,0:T(8,128)(2,1)S(1)} all-gather(bf16[1,6,2592]{2,1,0:T(8,128)(2,1)S(1)} %bitcast.288), channel_id=1, replica_groups=mesh['ha'=16,'wa'=16] {'ha'}, dimensions={0}, use_global_device_ids=true | all-gather | bytes 528768 | tf_op jit(solution)/shard_map/all_gather | solution.py:34
  62.7 1.9 collective-permute-start.6
  64.7 2.4 collective-permute-start.7
  67.9 1.9 collective-permute-done.7
  72.8 1.2 fusion.1
  74.1 1.4 copy.21
  76.5 1.7 fusion.11
  78.2 2.0 collective-permute-start
  80.2 1.3 collective-permute-start.1
  81.9 4.1 %collective-permute-done.1 = bf16[3,1,40,96]{3,2,1,0:T(8,128)(2,1)S(1)} collective-permute-done((bf16[3,1,40,96]{3,2,1,0:T(8,128)(2,1)S(1)}, bf16[3,1,40,96]{3,2,1,0:T(8,128)(2,1)S(1)}, u32[]{:S(2)}, u32[]{:S(2)}) %collective-permute-start.1) | collective-permute-done | bytes 23072 | tf_op jit(solution)/shard_map/ppermute | solution.py:15
  86.8 1.2 fusion.47
  89.1 1.0 convolution_bitcast_fusion.18
  90.1 1.0 convolution_bitcast_fusion.7
  91.2 1.9 collective-permute-start.2
  93.1 3.8 %collective-permute-start.3 = (bf16[3,47,1,96]{3,2,1,0:T(2,128)(2,1)S(1)}, bf16[3,47,1,96]{3,2,1,0:T(2,128)(2,1)S(1)}, u32[]{:S(2)}, u32[]{:S(2)}) collective-permute-start(bf16[3,47,1,96]{3,2,1,0:T(2,128)(2,1)S(1)} %get-tuple-element.24), channel_id=1, source_target_pairs={{1,0},{2,1},{3,2},{4,3},{5,4},{6,5},{7,6},{8,7},{9,8},{10,9},{11,1... | collective-permute-start | bytes 81224 | tf_op jit(solution)/shard_map/ppermute | solution.py:15
  97.9 1.5 collective-permute-done.3
  99.3 2.3 maximum_maximum_fusion
  101.7 2.4 fusion.74
  104.2 1.4 convolution_bitcast_fusion.17
  105.6 2.0 fusion.39
  107.6 1.0 convolution_bitcast_fusion.14
  108.5 1.9 fusion.35
  110.5 1.0 convolution_bitcast_fusion.9
  111.4 2.0 fusion.28
  113.4 1.0 convolution_bitcast_fusion.6
  114.4 1.9 fusion.67
  116.3 1.0 convolution_bitcast_fusion
  117.3 2.0 fusion.53
  119.3 1.0 convolution_bitcast_fusion.11
  120.2 1.0 convolution_bitcast_fusion.12
  121.2 1.0 convolution_bitcast_fusion.13
  122.1 1.0 convolution_bitcast_fusion.16
  123.1 1.0 convolution_bitcast_fusion.19
  126.0 1.0 convolution_bitcast_fusion.21
  126.9 1.0 convolution_bitcast_fusion.22
  127.9 1.0 convolution_bitcast_fusion.24
  129.8 1.0 convolution_bitcast_fusion.5
  130.8 1.0 convolution_bitcast_fusion.8
  131.7 2.2 concatenate.73
  134.0 1.5 convolution_add_fusion.26
  149.1 99.8 %all-reduce.4.cloned.1.call-done = f32[96,2592]{1,0:T(8,128)} async-done(((f32[96,2592]{1,0:T(8,128)}), f32[96,2592]{1,0:T(8,128)}) %all-reduce.4.cloned.1.call-update) | async-done | bytes 995344
  248.9 1.0 constant_dynamic-slice_fusion.1
  249.9 75.2 %all-reduce.1 = f32[96,162]{1,0:T(8,128)S(1)} all-reduce(f32[96,162]{1,0:T(8,128)S(1)} %constant_dynamic-slice_fusion.1), channel_id=3, replica_groups=mesh['ha'=16,'wa'=16] {'ha'}, use_global_device_ids=true, to_apply=%region_3.4.clone | all-reduce | flops 15552 | bytes 124416
  (157 shorter events, 27.9 us)
Async XLA Ops:
  7.2 24.5 %copy-start = (bf16[45,40,96]{2,1,0:T(8,128)(2,1)S(1)}, bf16[45,40,96]{2,1,0:T(8,128)(2,1)}, u32[]{:S(2)}) copy-start(bf16[45,40,96]{2,1,0:T(8,128)(2,1)} %param.11) | copy-start | bytes 1036804
  7.2 241.7 %all-reduce.4.cloned.1.call-start = ((), (), s32[]{:S(2)}) async-start(), calls=%async_computation | async-start | bytes 2064384
  8.0 54.4 %collective-permute-start.4 = (bf16[1,40,96]{2,1,0:T(8,128)(2,1)S(1)}, bf16[1,40,96]{2,1,0:T(8,128)(2,1)S(1)}, u32[]{:S(2)}, u32[]{:S(2)}) collective-permute-start(bf16[1,40,96]{2,1,0:T(8,128)(2,1)S(1)} %get-tuple-element.54), channel_id=1, source_target_pairs={{0,16},{16,32},{32,48},{48,64},{64,80},{80,96},{96,112},{112,128},... | collective-permute-start | bytes 23048 | tf_op jit(solution)/shard_map/ppermute | solution.py:12
  11.4 51.0 %collective-permute-start.5 = (bf16[1,40,96]{2,1,0:T(8,128)(2,1)S(1)}, bf16[1,40,96]{2,1,0:T(8,128)(2,1)S(1)}, u32[]{:S(2)}, u32[]{:S(2)}) collective-permute-start(bf16[1,40,96]{2,1,0:T(8,128)(2,1)S(1)} %get-tuple-element.53), channel_id=1, source_target_pairs={{16,0},{32,16},{48,32},{64,48},{80,64},{96,80},{112,96},{128,112},... | collective-permute-start | bytes 23048 | tf_op jit(solution)/shard_map/ppermute | solution.py:15
  30.6 29.2 %copy-start.45 = (u32[256]{0:T(256)S(1)}, u32[256]{0:T(256)}, u32[]{:S(2)}) copy-start(u32[256]{0:T(256)} %constant.21) | copy-start | bytes 3076
  30.6 29.9 %copy-start.44 = (u32[256]{0:T(256)S(1)}, u32[256]{0:T(256)}, u32[]{:S(2)}) copy-start(u32[256]{0:T(256)} %constant.25) | copy-start | bytes 3076
  59.8 27.0 %copy-start.35 = (bf16[96,2592]{1,0:T(8,128)(2,1)}, bf16[96,2592]{1,0:T(8,128)(2,1)S(1)}, u32[]{:S(2)}) copy-start(bf16[96,2592]{1,0:T(8,128)(2,1)S(1)} %reshape.72) | copy-start | bytes 1492996
  62.7 5.2 %collective-permute-start.6 = (bf16[47,1,96]{2,1,0:T(2,128)(2,1)S(1)}, bf16[47,1,96]{2,1,0:T(2,128)(2,1)S(1)}, u32[]{:S(2)}, u32[]{:S(2)}) collective-permute-start(bf16[47,1,96]{2,1,0:T(2,128)(2,1)S(1)} %get-tuple-element.48), channel_id=1, source_target_pairs={{1,0},{2,1},{3,2},{4,3},{5,4},{6,5},{7,6},{8,7},{9,8},{10,9},{11,1... | collective-permute-start | bytes 27080 | tf_op jit(solution)/shard_map/ppermute | solution.py:15
  64.7 5.1 %collective-permute-start.7 = (bf16[47,1,96]{2,1,0:T(2,128)(2,1)S(1)}, bf16[47,1,96]{2,1,0:T(2,128)(2,1)S(1)}, u32[]{:S(2)}, u32[]{:S(2)}) collective-permute-start(bf16[47,1,96]{2,1,0:T(2,128)(2,1)S(1)} %get-tuple-element.49), channel_id=1, source_target_pairs={{0,1},{1,2},{2,3},{3,4},{4,5},{5,6},{6,7},{7,8},{8,9},{9,10},{10,1... | collective-permute-start | bytes 27080 | tf_op jit(solution)/shard_map/ppermute | solution.py:12
  72.8 2.7 copy-start.2
  72.8 2.7 copy-start.42
  76.4 1.7 copy-start.1
  78.2 3.7 %collective-permute-start = (bf16[3,1,40,96]{3,2,1,0:T(8,128)(2,1)S(1)}, bf16[3,1,40,96]{3,2,1,0:T(8,128)(2,1)S(1)}, u32[]{:S(2)}, u32[]{:S(2)}) collective-permute-start(bf16[3,1,40,96]{3,2,1,0:T(8,128)(2,1)S(1)} %get-tuple-element.34), channel_id=1, source_target_pairs={{0,16},{16,32},{32,48},{48,64},{64,80},{80,96},{96,112},{112,128},... | collective-permute-start | bytes 69128 | tf_op jit(solution)/shard_map/ppermute | solution.py:12
  80.2 5.8 %collective-permute-start.1 = (bf16[3,1,40,96]{3,2,1,0:T(8,128)(2,1)S(1)}, bf16[3,1,40,96]{3,2,1,0:T(8,128)(2,1)S(1)}, u32[]{:S(2)}, u32[]{:S(2)}) collective-permute-start(bf16[3,1,40,96]{3,2,1,0:T(8,128)(2,1)S(1)} %get-tuple-element.35), channel_id=1, source_target_pairs={{16,0},{32,16},{48,32},{64,48},{80,64},{96,80},{112,96},{128,112},... | collective-permute-start | bytes 69128 | tf_op jit(solution)/shard_map/ppermute | solution.py:15
  86.4 2.3 copy-start.3
  86.4 2.3 copy-start.5
  86.5 2.6 copy-start.7
  86.5 10.5 %copy-start.9 = (bf16[1,45,40,96]{3,2,1,0:T(8,128)(2,1)}, bf16[1,45,40,96]{3,2,1,0:T(8,128)(2,1)S(1)}, u32[]{:S(2)}) copy-start(bf16[1,45,40,96]{3,2,1,0:T(8,128)(2,1)S(1)} %get-tuple-element.36) | copy-start | bytes 1036804
  91.2 6.7 %collective-permute-start.2 = (bf16[3,47,1,96]{3,2,1,0:T(2,128)(2,1)S(1)}, bf16[3,47,1,96]{3,2,1,0:T(2,128)(2,1)S(1)}, u32[]{:S(2)}, u32[]{:S(2)}) collective-permute-start(bf16[3,47,1,96]{3,2,1,0:T(2,128)(2,1)S(1)} %get-tuple-element.23), channel_id=1, source_target_pairs={{0,1},{1,2},{2,3},{3,4},{4,5},{5,6},{6,7},{7,8},{8,9},{9,10},{10,1... | collective-permute-start | bytes 81224 | tf_op jit(solution)/shard_map/ppermute | solution.py:12
  93.1 6.2 %collective-permute-start.3 = (bf16[3,47,1,96]{3,2,1,0:T(2,128)(2,1)S(1)}, bf16[3,47,1,96]{3,2,1,0:T(2,128)(2,1)S(1)}, u32[]{:S(2)}, u32[]{:S(2)}) collective-permute-start(bf16[3,47,1,96]{3,2,1,0:T(2,128)(2,1)S(1)} %get-tuple-element.24), channel_id=1, source_target_pairs={{1,0},{2,1},{3,2},{4,3},{5,4},{6,5},{7,6},{8,7},{9,8},{10,9},{11,1... | collective-permute-start | bytes 81224 | tf_op jit(solution)/shard_map/ppermute | solution.py:15
  104.1 15.2 %copy-start.19 = (bf16[1,45,40,96]{3,2,1,0:T(8,128)(2,1)}, bf16[1,45,40,96]{3,2,1,0:T(8,128)(2,1)S(1)}, u32[]{:S(2)}) copy-start(bf16[1,45,40,96]{3,2,1,0:T(8,128)(2,1)S(1)} %get-tuple-element.6) | copy-start | bytes 1036804
  104.1 16.1 %copy-start.21 = (bf16[1,45,40,96]{3,2,1,0:T(8,128)(2,1)}, bf16[1,45,40,96]{3,2,1,0:T(8,128)(2,1)S(1)}, u32[]{:S(2)}) copy-start(bf16[1,45,40,96]{3,2,1,0:T(8,128)(2,1)S(1)} %get-tuple-element.59) | copy-start | bytes 1036804
  104.1 17.1 %copy-start.23 = (bf16[1,45,40,96]{3,2,1,0:T(8,128)(2,1)}, bf16[1,45,40,96]{3,2,1,0:T(8,128)(2,1)S(1)}, u32[]{:S(2)}) copy-start(bf16[1,45,40,96]{3,2,1,0:T(8,128)(2,1)S(1)} %get-tuple-element.7) | copy-start | bytes 1036804
  104.1 18.0 %copy-start.25 = (bf16[1,45,40,96]{3,2,1,0:T(8,128)(2,1)}, bf16[1,45,40,96]{3,2,1,0:T(8,128)(2,1)S(1)}, u32[]{:S(2)}) copy-start(bf16[1,45,40,96]{3,2,1,0:T(8,128)(2,1)S(1)} %get-tuple-element.8) | copy-start | bytes 1036804
  104.1 19.0 %copy-start.27 = (bf16[1,45,40,96]{3,2,1,0:T(8,128)(2,1)}, bf16[1,45,40,96]{3,2,1,0:T(8,128)(2,1)S(1)}, u32[]{:S(2)}) copy-start(bf16[1,45,40,96]{3,2,1,0:T(8,128)(2,1)S(1)} %get-tuple-element.9) | copy-start | bytes 1036804
  104.1 19.9 %copy-start.11 = (bf16[1,45,40,96]{3,2,1,0:T(8,128)(2,1)}, bf16[1,45,40,96]{3,2,1,0:T(8,128)(2,1)S(1)}, u32[]{:S(2)}) copy-start(bf16[1,45,40,96]{3,2,1,0:T(8,128)(2,1)S(1)} %get-tuple-element.3) | copy-start | bytes 1036804
  104.1 20.9 %copy-start.29 = (bf16[1,45,40,96]{3,2,1,0:T(8,128)(2,1)}, bf16[1,45,40,96]{3,2,1,0:T(8,128)(2,1)S(1)}, u32[]{:S(2)}) copy-start(bf16[1,45,40,96]{3,2,1,0:T(8,128)(2,1)S(1)} %get-tuple-element.56) | copy-start | bytes 1036804
  104.2 21.8 %copy-start.31 = (bf16[1,45,40,96]{3,2,1,0:T(8,128)(2,1)}, bf16[1,45,40,96]{3,2,1,0:T(8,128)(2,1)S(1)}, u32[]{:S(2)}) copy-start(bf16[1,45,40,96]{3,2,1,0:T(8,128)(2,1)S(1)} %get-tuple-element.10) | copy-start | bytes 1036804
  104.2 22.8 %copy-start.33 = (bf16[1,45,40,96]{3,2,1,0:T(8,128)(2,1)}, bf16[1,45,40,96]{3,2,1,0:T(8,128)(2,1)S(1)}, u32[]{:S(2)}) copy-start(bf16[1,45,40,96]{3,2,1,0:T(8,128)(2,1)S(1)} %get-tuple-element.55) | copy-start | bytes 1036804
  104.2 24.7 %copy-start.13 = (bf16[1,45,40,96]{3,2,1,0:T(8,128)(2,1)}, bf16[1,45,40,96]{3,2,1,0:T(8,128)(2,1)S(1)}, u32[]{:S(2)}) copy-start(bf16[1,45,40,96]{3,2,1,0:T(8,128)(2,1)S(1)} %get-tuple-element.63) | copy-start | bytes 1036804
  104.2 25.6 %copy-start.15 = (bf16[1,45,40,96]{3,2,1,0:T(8,128)(2,1)}, bf16[1,45,40,96]{3,2,1,0:T(8,128)(2,1)S(1)}, u32[]{:S(2)}) copy-start(bf16[1,45,40,96]{3,2,1,0:T(8,128)(2,1)S(1)} %get-tuple-element.4) | copy-start | bytes 1036804
  104.2 26.6 %copy-start.17 = (bf16[1,45,40,96]{3,2,1,0:T(8,128)(2,1)}, bf16[1,45,40,96]{3,2,1,0:T(8,128)(2,1)S(1)}, u32[]{:S(2)}) copy-start(bf16[1,45,40,96]{3,2,1,0:T(8,128)(2,1)S(1)} %get-tuple-element.5) | copy-start | bytes 1036804
  134.0 1.6 copy-start.34
  134.0 1.6 copy-start.36
  134.0 1.9 copy-start.32
  136.3 1.1 copy-start.28
  137.0 1.1 copy-start.8
  137.0 1.3 copy-start.41
  138.3 1.4 copy-start.6
  138.3 1.4 copy-start.40
  139.7 1.3 copy-start.10
  140.7 1.1 copy-start.22
  141.0 1.1 copy-start.20
  141.7 1.1 copy-start.4
  141.7 1.3 copy-start.39
  143.0 1.4 copy-start.38
  145.7 1.1 copy-start.12
  146.4 1.1 copy-start.37
  (7 other events, 6.8 us)
Sparse Core Ops, SparseCore 0:
  134.1 114.6 all-reduce.3
where the time goes:
time: 334 us; the launch traced here: 333 us
  blocking collectives  119 us (36%)
  waiting for transfers between devices  107 us (32%)
  matrix products  46 us (14%)
  starting transfers between devices  18.1 us (5%)
  local copies, waits for them, and re-layouts  17.2 us (5%)
  between operations  16.2 us (5%)
  other arithmetic  8.68 us (3%)
    unnamed x2, waiting for transfers between devices  99.8 us
    unnamed x1, blocking collectives  75.2 us
    all_gather x1, blocking collectives, local(): full_weight = lax.all_gather(weight_part, 'ha', axis=0, tiled=True)  27.5 us
    dot_general x27, matrix products, local(): lax.dot_general(grad_flat, slab_rows, (((0,), (0,)), ((), ())), preferred...  22.5 us
    dot_general x27, matrix products, local(): lax.dot_general(slab_rows, tap_weight, (((1,), (1,)), ((), ())), preferre...  19.1 us
    all_gather x1, blocking collectives, local(): weight_part = lax.all_gather(conv_weight, 'wa', axis=1, tiled=True)  16.4 us
    ppermute x4, starting transfers between devices, padded_2(): lax.ppermute(lax.slice_in_dim(block, block.shape[dim] - width, None, axis...  9.72 us
    unnamed x99, local copies, waits for them, and re-layouts  8.98 us
  transfers between devices with their start and end apart: 9, of which 4 were waited for; matrix products, arithmetic and copies ran while one was open for 5% of the time, Pallas kernels for 0%

commit v1 on v0

v1 whole, which is shorter than its diff:
```python
import jax
import jax.numpy as jnp
from jax import lax
from jax.experimental import pallas as pl
from jax.experimental.pallas import tpu as pltpu
from jax.sharding import PartitionSpec as P

MESH = pl.DeviceIdType.MESH
F32 = jnp.float32
BF16 = jnp.bfloat16

H = 45
W = 40
C = 96
PITCH = 48
LEAD = 16
FLAT = (H + 2) * PITCH
PIX = H * PITCH
SROWS = LEAD + FLAT + 16
BASE = LEAD + PITCH
KB = 162
HALF = 14 * 128
ROWS = 9
XY = [(dy, dx) for dy in range(4) for dx in range(4) if (dy, dx) != (0, 0)]
XY.sort(key=lambda p: -(min(p[0], 4 - p[0]) + min(p[1], 4 - p[1])))


def slot_of(tap):
    return [tap] if tap < 13 else [13, 14] if tap == 13 else [tap + 1]


def nt(a, b):
    return lax.dot_general(a, b, (((1,), (1,)), ((), ())), preferred_element_type=F32)


def nn(a, b):
    return lax.dot_general(a, b, (((1,), (0,)), ((), ())), preferred_element_type=F32)


def remote(src, dst, send, recv, device):
    return pltpu.make_async_remote_copy(
        src_ref=src, dst_ref=dst, send_sem=send, recv_sem=recv, device_id=device, device_id_type=MESH
    )


def kernel(
    lat_ref, cache_ref, gain_ref, bias_ref, w_ref, gout_ref,
    out_ref, glat_ref, gw_ref,
    S, FS, FG, GT, gpad,
    rowbuf, colsend, colbuf, cornsend, cornbuf,
    Wtmp, Wown, Wp, Wl, Wg, Wn, Wb,
    Rs, RC, SB, RA, T, PZ, RZ,
    row_s, row_r, col_s, col_r, corn_s, corn_r,
    wp_s, wp_r, wg_s, wg_r, wc_s, wc_r,
    rc_s, rc_r, ra_s, ra_r, rz_s, rz_r,
):
    a = lax.axis_index("ha")
    b = lax.axis_index("wa")
    y, x = a // 4, a % 4
    z, core = b // 2, b % 2
    up, down = (a + 15) % 16, (a + 1) % 16
    left, right = (b + 15) % 16, (b + 1) % 16

    barrier = pltpu.get_barrier_semaphore()
    partners = [(a, (b + d) % 16) for d in range(1, 16)]
    partners += [((a + d) % 16, b) for d in range(1, 16)]
    partners += [(v, h) for v in (up, down) for h in (left, right)]
    for p in partners:
        pl.semaphore_signal(barrier, inc=1, device_id=p, device_id_type=MESH)

    S[...] = jnp.zeros_like(S)
    gpad[...] = jnp.zeros_like(gpad)
    gpad[:, 0:C] = gain_ref[...]
    Wtmp[...] = jnp.zeros_like(Wtmp)
    Wtmp[0:6, 0:KB] = w_ref[...].astype(F32)
    Wown[...] = Wtmp[...].astype(BF16)

    @pl.loop(0, H)
    def _(h):
        row = pl.multiple_of(BASE + h * PITCH, 8)
        S[0, pl.ds(row, W), 0:C] = cache_ref[0, h].astype(F32)
        S[1, pl.ds(row, W), 0:C] = cache_ref[1, h].astype(F32)
        S[2, pl.ds(row, W), 0:C] = lat_ref[h].astype(F32)
        S[3, pl.ds(row, W), 0:C] = gout_ref[h].astype(F32)

    for n in range(4):
        colsend[0, n, 0:H] = S[n, pl.ds(BASE, H, stride=PITCH)].astype(BF16)
        colsend[1, n, 0:H] = S[n, pl.ds(BASE + W - 1, H, stride=PITCH)].astype(BF16)
        for k, (r, c) in enumerate(((0, 0), (0, W - 1), (H - 1, 0), (H - 1, W - 1))):
            at = BASE + r * PITCH + c
            cornsend[k, n : n + 1] = S[n, at : at + 1]

    pl.semaphore_wait(barrier, len(partners))

    halo = []
    for k, (r, dev) in enumerate(((H - 1, (down, b)), (0, (up, b)))):
        for m, (src, dst) in enumerate(
            (
                (cache_ref.at[:, r], rowbuf.at[k, pl.ds(0, 2)]),
                (lat_ref.at[r], rowbuf.at[k, 2]),
                (gout_ref.at[r], rowbuf.at[k, 3]),
            )
        ):
            halo.append(remote(src, dst, row_s.at[k, m], row_r.at[k, m], dev))
    for k, dev in enumerate(((a, left), (a, right))):
        halo.append(remote(colsend.at[k], colbuf.at[k], col_s.at[k], col_r.at[k], dev))
    for k, dev in enumerate(((up, left), (up, right), (down, left), (down, right))):
        halo.append(remote(cornsend.at[k], cornbuf.at[k], corn_s.at[k], corn_r.at[k], dev))
    for copy in halo:
        copy.start()
    wpieces = [
        remote(Wown, Wp.at[b], wp_s.at[d - 1], wp_r.at[d - 1], (a, (b + d) % 16))
        for d in range(1, 16)
    ]
    for copy in wpieces:
        copy.start()
    Wp[b] = Wown[...]

    row_id = lax.broadcasted_iota(jnp.int32, (128, 128), 0)
    col_id = lax.broadcasted_iota(jnp.int32, (128, 128), 1)
    spread = (row_id % 8 < 6) & (col_id == (row_id // 8) * 6 + row_id % 8)
    spread = jnp.where(spread, 1.0, 0.0).astype(BF16)
    GT[...] = nt(spread, S[3, BASE : BASE + PIX].astype(BF16)).astype(BF16)

    for copy in halo:
        copy.wait_recv()
    for n in range(4):
        S[n, LEAD : LEAD + W, 0:C] = jnp.where(a > 0, rowbuf[0, n].astype(F32), 0.0)
        S[n, BASE + PIX : BASE + PIX + W, 0:C] = jnp.where(a < 15, rowbuf[1, n].astype(F32), 0.0)
        S[n, pl.ds(BASE + W, H, stride=PITCH)] = jnp.where(
            b < 15, colbuf[0, n, 0:H].astype(F32), 0.0
        )
        S[n, pl.ds(BASE - 1, H, stride=PITCH)] = jnp.where(
            b > 0, colbuf[1, n, 0:H].astype(F32), 0.0
        )
        for k, (at, there) in enumerate(
            (
                (BASE + PIX + W, (a < 15) & (b < 15)),
                (BASE + PIX - 1, (a < 15) & (b > 0)),
                (LEAD + W, (a > 0) & (b < 15)),
                (LEAD - 1, (a > 0) & (b > 0)),
            )
        ):
            S[n, at : at + 1] = jnp.where(there, cornbuf[k, n : n + 1], 0.0)

    gain = gpad[...]

    @pl.loop(0, SROWS // 176)
    def _(i):
        rows = pl.ds(pl.multiple_of(i * 176, 8), 176)
        v = S[2, rows]
        scale = lax.rsqrt(jnp.sum(v * v, axis=1, keepdims=True) * (1.0 / C) + 1e-06)
        n = v * scale * gain
        S[2, rows] = n / (1.0 + jnp.exp(-n))

    @pl.loop(0, 3)
    def _(i):
        at = pl.multiple_of(i * 752, 16)
        for n in range(4):
            block = S[n, pl.ds(at, 784)]
            for c in range(3):
                part = block[15 + c : 15 + c + 752].astype(BF16)
                k = 3 * c + n
                if n < 3:
                    FS[pl.ds(at, 752), k * 128 : (k + 1) * 128] = part
                else:
                    FG[pl.ds(at, 752), c * 128 : (c + 1) * 128] = part

    for copy in wpieces:
        copy.wait_recv()
    lane = lax.broadcasted_iota(jnp.int32, (8, 256), 1)
    for tap in range(27):
        total = jnp.zeros((8, 256), F32)
        for j in range(16):
            shift = KB * j - C * tap
            lo, hi = max(0, shift), min(C, shift + KB)
            if lo < hi:
                moved = pltpu.roll(Wp[j].astype(F32), shift % 256, 1)
                total += jnp.where((lane >= lo) & (lane < hi), moved, 0.0)
        for s in slot_of(tap):
            Wl[:, s * 128 : (s + 1) * 128] = total[:, 0:128].astype(BF16)
    mine = pl.ds(pl.multiple_of(core * HALF, 128), HALF)
    other = pl.ds(pl.multiple_of((1 - core) * HALF, 128), HALF)
    peers = [((y + dy) % 4 * 4 + (x + dx) % 4, b) for dy, dx in XY]
    partner = (a, z * 2 + 1 - core)
    wsends = [
        remote(Wl.at[:, mine], Wg.at[a, :, mine], wg_s.at[k], wg_r.at[k], p)
        for k, p in enumerate(peers)
    ]
    for copy in wsends:
        copy.start()
    Wg[a, :, mine] = Wl[:, mine]

    for r in range(3):
        part = nn(GT[...], FS[PITCH * r : PITCH * r + PIX])
        for c in range(3):
            for t in range(3):
                k = 3 * c + t
                block = part[:, k * 128 : (k + 1) * 128].reshape(16, 8, 128)
                for s in slot_of(9 * t + 3 * r + c):
                    Rs[:, :, s * 128 : (s + 1) * 128] = block
    pair = remote(Rs.at[:, :, other], RC, rc_s, rc_r, partner)
    pair.start()

    for copy in wsends:
        copy.wait_recv()
    wswap = remote(Wg.at[:, :, mine], Wg.at[:, :, mine], wc_s, wc_r, partner)
    wswap.start()

    pair.wait_recv()

    @pl.loop(0, 16)
    def _(k):
        SB[k] = (Rs[k, :, mine] + RC[k]).astype(SB.dtype)

    asends = [
        remote(SB.at[p[0]], RA.at[k], ra_s.at[k], ra_r.at[k], p) for k, p in enumerate(peers)
    ]
    for copy in asends:
        copy.start()

    wswap.wait()
    compact = (row_id < C) & (col_id == (row_id // 6) * 8 + row_id % 6)
    compact = jnp.where(compact, 1.0, 0.0).astype(BF16)
    for tap in range(27):
        s = slot_of(tap)[0]
        block = Wg[:, :, s * 128 : (s + 1) * 128].astype(F32).reshape(128, 128)
        block = nn(compact, block.astype(BF16)).astype(BF16)
        t, r, c = tap // 9, tap // 3 % 3, tap % 3
        Wn[r, :, (3 * c + t) * 128 : (3 * c + t + 1) * 128] = block
        if t == 2:
            Wb[r, (2 - c) * 128 : (3 - c) * 128] = block

    @pl.loop(0, H // ROWS)
    def _(i):
        h0 = i * ROWS
        at = pl.multiple_of(h0 * PITCH, 16)
        acc = nt(FS[pl.ds(at, ROWS * PITCH)], Wn[0])
        acc += nt(FS[pl.ds(at + PITCH, ROWS * PITCH)], Wn[1])
        acc += nt(FS[pl.ds(at + 2 * PITCH, ROWS * PITCH)], Wn[2])
        acc = acc.reshape(ROWS, PITCH, 128)[:, 0:W, 0:C]
        lat = lat_ref[pl.ds(h0, ROWS)].astype(F32)
        out_ref[pl.ds(h0, ROWS)] = (lat + bias_ref[...].reshape(1, 1, C) + acc).astype(BF16)

        back = nn(FG[pl.ds(at + 2 * PITCH, ROWS * PITCH)], Wb[0])
        back += nn(FG[pl.ds(at + PITCH, ROWS * PITCH)], Wb[1])
        back += nn(FG[pl.ds(at, ROWS * PITCH)], Wb[2])
        dact = back.reshape(ROWS, PITCH, 128)[:, 0:W, 0:C]
        g = gain_ref[...].reshape(1, 1, C)
        scale = lax.rsqrt(jnp.sum(lat * lat, axis=2, keepdims=True) * (1.0 / C) + 1e-06)
        n = lat * scale * g
        sig = 1.0 / (1.0 + jnp.exp(-n))
        du = dact * (sig * (1.0 + n * (1.0 - sig))) * g
        inner = jnp.sum(lat * du, axis=2, keepdims=True) * (1.0 / C)
        dlat = scale * du - lat * (scale * scale * scale * inner)
        glat_ref[pl.ds(h0, ROWS)] = (gout_ref[pl.ds(h0, ROWS)].astype(F32) + dlat).astype(BF16)

    total = Rs[a, :, mine] + RC[a]
    for k, copy in enumerate(asends):
        copy.wait_recv()
        total += RA[k].astype(F32)
    T[...] = total
    for half in range(2):

        @pl.when(core == half)
        def _():
            for j in range(8):
                piece = jnp.zeros((8, 256), F32)
                for m in range(14):
                    shift = C * m - (KB * j + 48 * half)
                    lo, hi = max(0, shift), min(KB, shift + C)
                    if lo < hi:
                        block = jnp.concatenate(
                            [T[:, m * 128 : (m + 1) * 128], jnp.zeros((8, 128), F32)], axis=1
                        )
                        moved = pltpu.roll(block, shift % 256, 1)
                        piece += jnp.where((lane >= lo) & (lane < hi), moved, 0.0)
                PZ[j] = piece

    zsends = []
    for j in range(8):
        oz, oc = 4 * core + j // 2, j % 2
        itself = (oz == z) & (oc == core)
        copy = remote(PZ.at[j], RZ.at[z], rz_s.at[j], rz_r.at[z], (a, oz * 2 + oc))
        zsends.append((itself, copy))

        @pl.when(jnp.logical_not(itself))
        def _():
            copy.start()

        @pl.when(itself)
        def _():
            RZ[z] = PZ[j]

    for k in range(8):
        source = (a, k * 2 + z // 4)

        @pl.when(jnp.logical_not((k == z) & (z // 4 == core)))
        def _():
            remote(PZ.at[0], RZ.at[k], rz_s.at[0], rz_r.at[k], source).wait_recv()

    final = RZ[0]
    for k in range(1, 8):
        final += RZ[k]
    gw_ref[...] = final[0:6, 0:KB]

    for copy in halo + wpieces + wsends + asends:
        copy.wait_send()
    pair.wait_send()
    for itself, copy in zsends:

        @pl.when(jnp.logical_not(itself))
        def _():
            copy.wait_send()


def local(latent, frame_cache, norm_gain, conv_bias, conv_weight, grad_out):
    vmem = pl.BlockSpec(memory_space=pltpu.VMEM)
    dma = pltpu.SemaphoreType.DMA
    return pl.pallas_call(
        kernel,
        out_shape=(
            jax.ShapeDtypeStruct((H, W, C), BF16),
            jax.ShapeDtypeStruct((H, W, C), BF16),
            jax.ShapeDtypeStruct((6, KB), F32),
        ),
        in_specs=[vmem] * 6,
        out_specs=(vmem, vmem, vmem),
        scratch_shapes=[
            pltpu.VMEM((4, SROWS, 128), F32),
            pltpu.VMEM((FLAT, 9 * 128), BF16),
            pltpu.VMEM((FLAT, 3 * 128), BF16),
            pltpu.VMEM((128, PIX), BF16),
            pltpu.VMEM((1, 128), F32),
            pltpu.VMEM((2, 4, W, C), BF16),
            pltpu.VMEM((2, 4, 48, 128), BF16),
            pltpu.VMEM((2, 4, 48, 128), BF16),
            pltpu.VMEM((4, 8, 128), F32),
            pltpu.VMEM((4, 8, 128), F32),
            pltpu.VMEM((8, 256), F32),
            pltpu.VMEM((8, 256), BF16),
            pltpu.VMEM((16, 8, 256), BF16),
            pltpu.VMEM((8, 2 * HALF), BF16),
            pltpu.VMEM((16, 8, 2 * HALF), BF16),
            pltpu.VMEM((3, 128, 9 * 128), BF16),
            pltpu.VMEM((3, 3 * 128, 128), BF16),
            pltpu.VMEM((16, 8, 2 * HALF), F32),
            pltpu.VMEM((16, 8, HALF), F32),
            pltpu.VMEM((16, 8, HALF), F32),
            pltpu.VMEM((15, 8, HALF), F32),
            pltpu.VMEM((8, HALF), F32),
            pltpu.VMEM((8, 8, 256), F32),
            pltpu.VMEM((8, 8, 256), F32),
            dma((2, 3)), dma((2, 3)), dma((2,)), dma((2,)), dma((4,)), dma((4,)),
            dma((15,)), dma((15,)), dma((15,)), dma((15,)), dma, dma,
            dma, dma, dma((15,)), dma((15,)), dma((8,)), dma((8,)),
        ],
        compiler_params=pltpu.CompilerParams(
            collective_id=0, has_side_effects=True, vmem_limit_bytes=60 * 1024 * 1024
        ),
    )(
        latent, frame_cache, norm_gain.reshape(1, C), conv_bias.reshape(1, C), conv_weight, grad_out
    )


def solution(mesh):
    placed = (
        P("ha", "wa", None),
        P(None, "ha", "wa", None),
        P(),
        P(),
        P("ha", "wa"),
        P("ha", "wa", None),
    )
    return jax.shard_map(
        local,
        mesh=mesh,
        in_specs=placed,
        out_specs=(P("ha", "wa", None), P("ha", "wa", None), P("ha", "wa")),
        check_vma=False,
    )
```

time: 334 us -> 53 us (0.16)
  the two profiles are of different devices: /device:TPU:96 before, /device:TPU:1 now
where the time goes in v1:
time: 53 us; the launch traced here: 52.9 us
  Pallas kernels  49 us (92%)
  local copies, waits for them, and re-layouts  3.26 us (6%)
  between operations  0.65 us (1%)
    pallas_call x1, Pallas kernels, local(): pl.pallas_call(kernel, out_shape=(jax.ShapeDtypeStruct((H, W, C), BF16),...  49 us
    unnamed x7, local copies, waits for them, and re-layouts  3.26 us

profile of v1, /device:TPU:1, one launch (start us, length us, event | category | flops | bytes accessed | tf_op | source)
XLA Modules:
  0.0 52.9 jit_solution(6200042390626084138)
XLA Ops:
  0.6 49.0 %shard_map.85 = (bf16[45,40,96]{2,1,0:T(8,128)(2,1)}, bf16[45,40,96]{2,1,0:T(8,128)(2,1)}, f32[6,162]{1,0:T(8,128)}) custom-call(bf16[45,40,96]{2,1,0:T(8,128)(2,1)} %lat_ref.1, bf16[2,45,40,96]{3,2,1,0:T(8,128)(2,1)} %cache_ref.1, f32[1,96]{1,0:T(1,128)} %bitcast.2, f32[1,96]{1,0:T(1,128)} %bitcast.3, bf16[6,162]{1,0:T(8,128)(2,1)} %w_ref.1, ...), custom_call_target="tpu_custom_call" | custom-call | tf_op jit(solution)/shard_map/pallas_call | solution.py:320
  49.6 0.0 copy-start
  49.6 1.9 %copy.12 = bf16[45,40,96]{2,1,0:T(8,128)(2,1)} copy(bf16[45,40,96]{2,1,0:T(8,128)(2,1)} %get-tuple-element.6) | data formatting | bytes 691200
  51.5 0.0 copy-done
  51.5 0.0 copy-start.1
  51.5 0.8 %copy.13 = bf16[45,40,96]{2,1,0:T(8,128)(2,1)} copy(bf16[45,40,96]{2,1,0:T(8,128)(2,1)S(1)} %copy-done) | data formatting | bytes 691200
  52.3 0.0 copy-done.1
  52.3 0.6 %copy.14 = f32[6,162]{1,0:T(8,128)} copy(f32[6,162]{1,0:T(8,128)S(1)} %copy-done.1) | data formatting | bytes 7776
Async XLA Ops:
  49.6 1.9 %copy-start = (bf16[45,40,96]{2,1,0:T(8,128)(2,1)S(1)}, bf16[45,40,96]{2,1,0:T(8,128)(2,1)}, u32[]{:S(2)}) copy-start(bf16[45,40,96]{2,1,0:T(8,128)(2,1)} %get-tuple-element.7) | copy-start | bytes 1036804
  51.5 0.8 %copy-start.1 = (f32[6,162]{1,0:T(8,128)S(1)}, f32[6,162]{1,0:T(8,128)}, u32[]{:S(2)}) copy-start(f32[6,162]{1,0:T(8,128)} %get-tuple-element.8) | copy-start | bytes 11668

commit v2 on v1

--- a/solution.py
+++ b/solution.py
@@ -21,6 +21,7 @@
 KB = 162
 HALF = 14 * 128
 ROWS = 9
+EARLY = 3
 XY = [(dy, dx) for dy in range(4) for dx in range(4) if (dy, dx) != (0, 0)]
 XY.sort(key=lambda p: -(min(p[0], 4 - p[0]) + min(p[1], 4 - p[1])))
 
@@ -49,7 +50,7 @@
     S, FS, FG, GT, gpad,
     rowbuf, colsend, colbuf, cornsend, cornbuf,
     Wtmp, Wown, Wp, Wl, Wg, Wn, Wb,
-    Rs, RC, SB, RA, T, PZ, RZ,
+    Rs, RP, RC, SB, RA, T, PZ, RZ,
     row_s, row_r, col_s, col_r, corn_s, corn_r,
     wp_s, wp_r, wg_s, wg_r, wc_s, wc_r,
     rc_s, rc_r, ra_s, ra_r, rz_s, rz_r,
@@ -121,50 +122,6 @@
     spread = (row_id % 8 < 6) & (col_id == (row_id // 8) * 6 + row_id % 8)
     spread = jnp.where(spread, 1.0, 0.0).astype(BF16)
     GT[...] = nt(spread, S[3, BASE : BASE + PIX].astype(BF16)).astype(BF16)
-
-    for copy in halo:
-        copy.wait_recv()
-    for n in range(4):
-        S[n, LEAD : LEAD + W, 0:C] = jnp.where(a > 0, rowbuf[0, n].astype(F32), 0.0)
-        S[n, BASE + PIX : BASE + PIX + W, 0:C] = jnp.where(a < 15, rowbuf[1, n].astype(F32), 0.0)
-        S[n, pl.ds(BASE + W, H, stride=PITCH)] = jnp.where(
-            b < 15, colbuf[0, n, 0:H].astype(F32), 0.0
-        )
-        S[n, pl.ds(BASE - 1, H, stride=PITCH)] = jnp.where(
-            b > 0, colbuf[1, n, 0:H].astype(F32), 0.0
-        )
-        for k, (at, there) in enumerate(
-            (
-                (BASE + PIX + W, (a < 15) & (b < 15)),
-                (BASE + PIX - 1, (a < 15) & (b > 0)),
-                (LEAD + W, (a > 0) & (b < 15)),
-                (LEAD - 1, (a > 0) & (b > 0)),
-            )
-        ):
-            S[n, at : at + 1] = jnp.where(there, cornbuf[k, n : n + 1], 0.0)
-
-    gain = gpad[...]
-
-    @pl.loop(0, SROWS // 176)
-    def _(i):
-        rows = pl.ds(pl.multiple_of(i * 176, 8), 176)
-        v = S[2, rows]
-        scale = lax.rsqrt(jnp.sum(v * v, axis=1, keepdims=True) * (1.0 / C) + 1e-06)
-        n = v * scale * gain
-        S[2, rows] = n / (1.0 + jnp.exp(-n))
-
-    @pl.loop(0, 3)
-    def _(i):
-        at = pl.multiple_of(i * 752, 16)
-        for n in range(4):
-            block = S[n, pl.ds(at, 784)]
-            for c in range(3):
-                part = block[15 + c : 15 + c + 752].astype(BF16)
-                k = 3 * c + n
-                if n < 3:
-                    FS[pl.ds(at, 752), k * 128 : (k + 1) * 128] = part
-                else:
-                    FG[pl.ds(at, 752), c * 128 : (c + 1) * 128] = part
 
     for copy in wpieces:
         copy.wait_recv()
@@ -191,6 +148,48 @@
         copy.start()
     Wg[a, :, mine] = Wl[:, mine]
 
+    for copy in halo:
+        copy.wait_recv()
+    for n in range(4):
+        S[n, LEAD : LEAD + W, 0:C] = jnp.where(a > 0, rowbuf[0, n].astype(F32), 0.0)
+        S[n, BASE + PIX : BASE + PIX + W, 0:C] = jnp.where(a < 15, rowbuf[1, n].astype(F32), 0.0)
+        S[n, pl.ds(BASE + W, H, stride=PITCH)] = jnp.where(
+            b < 15, colbuf[0, n, 0:H].astype(F32), 0.0
+        )
+        S[n, pl.ds(BASE - 1, H, stride=PITCH)] = jnp.where(
+            b > 0, colbuf[1, n, 0:H].astype(F32), 0.0
+        )
+        for k, (at, there) in enumerate(
+            (
+                (BASE + PIX + W, (a < 15) & (b < 15)),
+                (BASE + PIX - 1, (a < 15) & (b > 0)),
+                (LEAD + W, (a > 0) & (b < 15)),
+                (LEAD - 1, (a > 0) & (b > 0)),
+            )
+        ):
+            S[n, at : at + 1] = jnp.where(there, cornbuf[k, n : n + 1], 0.0)
+
+    gain = gpad[...]
+
+    @pl.loop(0, SROWS // 176)
+    def _(i):
+        rows = pl.ds(pl.multiple_of(i * 176, 8), 176)
+        v = S[2, rows]
+        scale = lax.rsqrt(jnp.sum(v * v, axis=1, keepdims=True) * (1.0 / C) + 1e-06)
+        n = v * scale * gain
+        S[2, rows] = n / (1.0 + jnp.exp(-n))
+
+    @pl.loop(0, 3)
+    def _(i):
+        at = pl.multiple_of(i * 752, 16)
+        for n in range(3):
+            block = S[n, pl.ds(at, 784)]
+            for c in range(3):
+                k = 3 * c + n
+                FS[pl.ds(at, 752), k * 128 : (k + 1) * 128] = block[15 + c : 15 + c + 752].astype(
+                    BF16
+                )
+
     for r in range(3):
         part = nn(GT[...], FS[PITCH * r : PITCH * r + PIX])
         for c in range(3):
@@ -199,19 +198,31 @@
                 block = part[:, k * 128 : (k + 1) * 128].reshape(16, 8, 128)
                 for s in slot_of(9 * t + 3 * r + c):
                     Rs[:, :, s * 128 : (s + 1) * 128] = block
-    pair = remote(Rs.at[:, :, other], RC, rc_s, rc_r, partner)
-    pair.start()
-
-    for copy in wsends:
-        copy.wait_recv()
-    wswap = remote(Wg.at[:, :, mine], Wg.at[:, :, mine], wc_s, wc_r, partner)
-    wswap.start()
-
-    pair.wait_recv()
+        if r == 1:
+            for copy in wsends:
+                copy.wait_recv()
+            wswap = remote(Wg.at[:, :, mine], Wg.at[:, :, mine], wc_s, wc_r, partner)
+            wswap.start()
 
     @pl.loop(0, 16)
     def _(k):
-        SB[k] = (Rs[k, :, mine] + RC[k]).astype(SB.dtype)
+        RP[k] = Rs[k, :, other].astype(BF16)
+
+    pair = remote(RP, RC, rc_s, rc_r, partner)
+    pair.start()
+
+    @pl.loop(0, 3)
+    def _(i):
+        at = pl.multiple_of(i * 752, 16)
+        block = S[3, pl.ds(at, 784)]
+        for c in range(3):
+            FG[pl.ds(at, 752), c * 128 : (c + 1) * 128] = block[15 + c : 15 + c + 752].astype(BF16)
+
+    pair.wait_recv()
+
+    @pl.loop(0, 16)
+    def _(k):
+        SB[k] = (Rs[k, :, mine] + RC[k].astype(F32)).astype(BF16)
 
     asends = [
         remote(SB.at[p[0]], RA.at[k], ra_s.at[k], ra_r.at[k], p) for k, p in enumerate(peers)
@@ -231,8 +242,7 @@
         if t == 2:
             Wb[r, (2 - c) * 128 : (3 - c) * 128] = block
 
-    @pl.loop(0, H // ROWS)
-    def _(i):
+    def rows_step(i):
         h0 = i * ROWS
         at = pl.multiple_of(h0 * PITCH, 16)
         acc = nt(FS[pl.ds(at, ROWS * PITCH)], Wn[0])
@@ -255,7 +265,9 @@
         dlat = scale * du - lat * (scale * scale * scale * inner)
         glat_ref[pl.ds(h0, ROWS)] = (gout_ref[pl.ds(h0, ROWS)].astype(F32) + dlat).astype(BF16)
 
-    total = Rs[a, :, mine] + RC[a]
+    pl.loop(0, EARLY)(rows_step)
+
+    total = Rs[a, :, mine] + RC[a].astype(F32)
     for k, copy in enumerate(asends):
         copy.wait_recv()
         total += RA[k].astype(F32)
@@ -291,6 +303,8 @@
         @pl.when(itself)
         def _():
             RZ[z] = PZ[j]
+
+    pl.loop(EARLY, H // ROWS)(rows_step)
 
     for k in range(8):
         source = (a, k * 2 + z // 4)
@@ -345,9 +359,10 @@
             pltpu.VMEM((3, 128, 9 * 128), BF16),
             pltpu.VMEM((3, 3 * 128, 128), BF16),
             pltpu.VMEM((16, 8, 2 * HALF), F32),
-            pltpu.VMEM((16, 8, HALF), F32),
-            pltpu.VMEM((16, 8, HALF), F32),
-            pltpu.VMEM((15, 8, HALF), F32),
+            pltpu.VMEM((16, 8, HALF), BF16),
+            pltpu.VMEM((16, 8, HALF), BF16),
+            pltpu.VMEM((16, 8, HALF), BF16),
+            pltpu.VMEM((15, 8, HALF), BF16),
             pltpu.VMEM((8, HALF), F32),
             pltpu.VMEM((8, 8, 256), F32),
             pltpu.VMEM((8, 8, 256), F32),

time: 53 us -> 48.1 us (0.908)
  Pallas kernels: 49 us -> 44.1 us
    pallas_call x1, Pallas kernels: 49 us -> 44.1 us  [local(): pl.pallas_call(kernel, out_shape=(jax.ShapeDtypeStruct((H, W, C), BF16),...]
where the time goes in v2:
time: 48.1 us; the launch traced here: 48 us
  Pallas kernels  44.1 us (92%)
  local copies, waits for them, and re-layouts  3.26 us (7%)
  between operations  0.65 us (1%)
    pallas_call x1, Pallas kernels, local(): pl.pallas_call(kernel, out_shape=(jax.ShapeDtypeStruct((H, W, C), BF16),...  44.1 us
    unnamed x7, local copies, waits for them, and re-layouts  3.26 us

profile of v2, /device:TPU:1, one launch (start us, length us, event | category | flops | bytes accessed | tf_op | source)
XLA Modules:
  0.0 48.0 jit_solution(7048980899006753542)
XLA Ops:
  0.6 44.1 %shard_map.85 = (bf16[45,40,96]{2,1,0:T(8,128)(2,1)}, bf16[45,40,96]{2,1,0:T(8,128)(2,1)}, f32[6,162]{1,0:T(8,128)}) custom-call(bf16[45,40,96]{2,1,0:T(8,128)(2,1)} %lat_ref.1, bf16[2,45,40,96]{3,2,1,0:T(8,128)(2,1)} %cache_ref.1, f32[1,96]{1,0:T(1,128)} %bitcast.2, f32[1,96]{1,0:T(1,128)} %bitcast.3, bf16[6,162]{1,0:T(8,128)(2,1)} %w_ref.1, ...), custom_call_target="tpu_custom_call" | custom-call | tf_op jit(solution)/shard_map/pallas_call | solution.py:334
  44.7 0.0 copy-start
  44.7 1.9 %copy.12 = bf16[45,40,96]{2,1,0:T(8,128)(2,1)} copy(bf16[45,40,96]{2,1,0:T(8,128)(2,1)} %get-tuple-element.6) | data formatting | bytes 691200
  46.6 0.0 copy-done
  46.6 0.0 copy-start.1
  46.6 0.8 %copy.13 = bf16[45,40,96]{2,1,0:T(8,128)(2,1)} copy(bf16[45,40,96]{2,1,0:T(8,128)(2,1)S(1)} %copy-done) | data formatting | bytes 691200
  47.4 0.0 copy-done.1
  47.4 0.6 %copy.14 = f32[6,162]{1,0:T(8,128)} copy(f32[6,162]{1,0:T(8,128)S(1)} %copy-done.1) | data formatting | bytes 7776
Async XLA Ops:
  44.7 1.9 %copy-start = (bf16[45,40,96]{2,1,0:T(8,128)(2,1)S(1)}, bf16[45,40,96]{2,1,0:T(8,128)(2,1)}, u32[]{:S(2)}) copy-start(bf16[45,40,96]{2,1,0:T(8,128)(2,1)} %get-tuple-element.7) | copy-start | bytes 1036804
  46.6 0.8 %copy-start.1 = (f32[6,162]{1,0:T(8,128)S(1)}, f32[6,162]{1,0:T(8,128)}, u32[]{:S(2)}) copy-start(f32[6,162]{1,0:T(8,128)} %get-tuple-element.8) | copy-start | bytes 11668

commit v3 on v2

--- a/solution.py
+++ b/solution.py
@@ -26,8 +26,20 @@
 XY.sort(key=lambda p: -(min(p[0], 4 - p[0]) + min(p[1], 4 - p[1])))
 
 
+ORDER = (
+    (0, 1, 2, 9, 10, 11, 3, 4, 5, 12, 13, 6, 7, 8),
+    (18, 19, 20, 13, 14, 21, 22, 23, 15, 16, 17, 24, 25, 26),
+)
+CHUNKS = ((0, 3), (3, 8), (8, 14))
+SUMS = ((0, 8), (8, 14))
+
+
 def slot_of(tap):
-    return [tap] if tap < 13 else [13, 14] if tap == 13 else [tap + 1]
+    return [14 * half + ORDER[half].index(tap) for half in (0, 1) if tap in ORDER[half]]
+
+
+def tiles(core, lo, hi):
+    return pl.ds(pl.multiple_of(core * HALF + lo * 128, 128), (hi - lo) * 128)
 
 
 def nt(a, b):
@@ -50,7 +62,7 @@
     S, FS, FG, GT, gpad,
     rowbuf, colsend, colbuf, cornsend, cornbuf,
     Wtmp, Wown, Wp, Wl, Wg, Wn, Wb,
-    Rs, RP, RC, SB, RA, T, PZ, RZ,
+    Rs, RC, SB, RA, T, PZ, RZ,
     row_s, row_r, col_s, col_r, corn_s, corn_r,
     wp_s, wp_r, wg_s, wg_r, wc_s, wc_r,
     rc_s, rc_r, ra_s, ra_r, rz_s, rz_r,
@@ -137,7 +149,6 @@
         for s in slot_of(tap):
             Wl[:, s * 128 : (s + 1) * 128] = total[:, 0:128].astype(BF16)
     mine = pl.ds(pl.multiple_of(core * HALF, 128), HALF)
-    other = pl.ds(pl.multiple_of((1 - core) * HALF, 128), HALF)
     peers = [((y + dy) % 4 * 4 + (x + dx) % 4, b) for dy, dx in XY]
     partner = (a, z * 2 + 1 - core)
     wsends = [
@@ -179,17 +190,12 @@
         n = v * scale * gain
         S[2, rows] = n / (1.0 + jnp.exp(-n))
 
-    @pl.loop(0, 3)
-    def _(i):
-        at = pl.multiple_of(i * 752, 16)
-        for n in range(3):
-            block = S[n, pl.ds(at, 784)]
-            for c in range(3):
-                k = 3 * c + n
-                FS[pl.ds(at, 752), k * 128 : (k + 1) * 128] = block[15 + c : 15 + c + 752].astype(
-                    BF16
-                )
-
+    for n in range(3):
+        for c in range(3):
+            k = 3 * c + n
+            FS[:, k * 128 : (k + 1) * 128] = S[n, 15 + c : 15 + c + FLAT].astype(BF16)
+
+    pairs = []
     for r in range(3):
         part = nn(GT[...], FS[PITCH * r : PITCH * r + PIX])
         for c in range(3):
@@ -198,37 +204,43 @@
                 block = part[:, k * 128 : (k + 1) * 128].reshape(16, 8, 128)
                 for s in slot_of(9 * t + 3 * r + c):
                     Rs[:, :, s * 128 : (s + 1) * 128] = block
+        lo, hi = CHUNKS[r]
+        pair = remote(
+            Rs.at[:, :, tiles(1 - core, lo, hi)],
+            RC.at[:, :, lo * 128 : hi * 128],
+            rc_s.at[r],
+            rc_r.at[r],
+            partner,
+        )
+        pair.start()
+        pairs.append(pair)
         if r == 1:
             for copy in wsends:
                 copy.wait_recv()
             wswap = remote(Wg.at[:, :, mine], Wg.at[:, :, mine], wc_s, wc_r, partner)
             wswap.start()
 
-    @pl.loop(0, 16)
-    def _(k):
-        RP[k] = Rs[k, :, other].astype(BF16)
-
-    pair = remote(RP, RC, rc_s, rc_r, partner)
-    pair.start()
-
-    @pl.loop(0, 3)
-    def _(i):
-        at = pl.multiple_of(i * 752, 16)
-        block = S[3, pl.ds(at, 784)]
-        for c in range(3):
-            FG[pl.ds(at, 752), c * 128 : (c + 1) * 128] = block[15 + c : 15 + c + 752].astype(BF16)
-
-    pair.wait_recv()
-
-    @pl.loop(0, 16)
-    def _(k):
-        SB[k] = (Rs[k, :, mine] + RC[k].astype(F32)).astype(BF16)
-
-    asends = [
-        remote(SB.at[p[0]], RA.at[k], ra_s.at[k], ra_r.at[k], p) for k, p in enumerate(peers)
-    ]
-    for copy in asends:
-        copy.start()
+    asends = []
+    for n, (lo, hi) in enumerate(SUMS):
+        lanes = slice(lo * 128, hi * 128)
+        if n == 0:
+            pairs[0].wait_recv()
+            pairs[1].wait_recv()
+        else:
+            for c in range(3):
+                FG[:, c * 128 : (c + 1) * 128] = S[3, 15 + c : 15 + c + FLAT].astype(BF16)
+            pairs[2].wait_recv()
+
+        @pl.loop(0, 16)
+        def _(k):
+            SB[k, :, lanes] = (Rs[k, :, tiles(core, lo, hi)] + RC[k, :, lanes]).astype(BF16)
+
+        for k, p in enumerate(peers):
+            copy = remote(
+                SB.at[p[0], :, lanes], RA.at[k, :, lanes], ra_s.at[n, k], ra_r.at[n, k], p
+            )
+            copy.start()
+            asends.append(copy)
 
     wswap.wait()
     compact = (row_id < C) & (col_id == (row_id // 6) * 8 + row_id % 6)
@@ -267,9 +279,10 @@
 
     pl.loop(0, EARLY)(rows_step)
 
-    total = Rs[a, :, mine] + RC[a].astype(F32)
-    for k, copy in enumerate(asends):
+    for copy in asends:
         copy.wait_recv()
+    total = Rs[a, :, mine] + RC[a]
+    for k in range(15):
         total += RA[k].astype(F32)
     T[...] = total
     for half in range(2):
@@ -282,8 +295,9 @@
                     shift = C * m - (KB * j + 48 * half)
                     lo, hi = max(0, shift), min(KB, shift + C)
                     if lo < hi:
+                        s = ORDER[half].index(13 * half + m)
                         block = jnp.concatenate(
-                            [T[:, m * 128 : (m + 1) * 128], jnp.zeros((8, 128), F32)], axis=1
+                            [T[:, s * 128 : (s + 1) * 128], jnp.zeros((8, 128), F32)], axis=1
                         )
                         moved = pltpu.roll(block, shift % 256, 1)
                         piece += jnp.where((lane >= lo) & (lane < hi), moved, 0.0)
@@ -318,9 +332,8 @@
         final += RZ[k]
     gw_ref[...] = final[0:6, 0:KB]
 
-    for copy in halo + wpieces + wsends + asends:
+    for copy in halo + wpieces + wsends + pairs + asends:
         copy.wait_send()
-    pair.wait_send()
     for itself, copy in zsends:
 
         @pl.when(jnp.logical_not(itself))
@@ -359,8 +372,7 @@
             pltpu.VMEM((3, 128, 9 * 128), BF16),
             pltpu.VMEM((3, 3 * 128, 128), BF16),
             pltpu.VMEM((16, 8, 2 * HALF), F32),
-            pltpu.VMEM((16, 8, HALF), BF16),
-            pltpu.VMEM((16, 8, HALF), BF16),
+            pltpu.VMEM((16, 8, HALF), F32),
             pltpu.VMEM((16, 8, HALF), BF16),
             pltpu.VMEM((15, 8, HALF), BF16),
             pltpu.VMEM((8, HALF), F32),
@@ -368,7 +380,7 @@
             pltpu.VMEM((8, 8, 256), F32),
             dma((2, 3)), dma((2, 3)), dma((2,)), dma((2,)), dma((4,)), dma((4,)),
             dma((15,)), dma((15,)), dma((15,)), dma((15,)), dma, dma,
-            dma, dma, dma((15,)), dma((15,)), dma((8,)), dma((8,)),
+            dma((3,)), dma((3,)), dma((2, 15)), dma((2, 15)), dma((8,)), dma((8,)),
         ],
         compiler_params=pltpu.CompilerParams(
             collective_id=0, has_side_effects=True, vmem_limit_bytes=60 * 1024 * 1024

time: 48.1 us -> 45.9 us (0.954)
  Pallas kernels: 44.1 us -> 41.9 us
    pallas_call x1, Pallas kernels: 44.1 us -> 41.9 us  [local(): pl.pallas_call(kernel, out_shape=(jax.ShapeDtypeStruct((H, W, C), BF16),...]
where the time goes in v3:
time: 45.9 us; the launch traced here: 45.8 us
  Pallas kernels  41.9 us (91%)
  local copies, waits for them, and re-layouts  3.26 us (7%)
  between operations  0.65 us (1%)
    pallas_call x1, Pallas kernels, local(): pl.pallas_call(kernel, out_shape=(jax.ShapeDtypeStruct((H, W, C), BF16),...  41.9 us
    unnamed x7, local copies, waits for them, and re-layouts  3.26 us

profile of v3, /device:TPU:1, one launch (start us, length us, event | category | flops | bytes accessed | tf_op | source)
XLA Modules:
  0.0 45.8 jit_solution(11400102656043624271)
XLA Ops:
  0.6 41.9 %shard_map.85 = (bf16[45,40,96]{2,1,0:T(8,128)(2,1)}, bf16[45,40,96]{2,1,0:T(8,128)(2,1)}, f32[6,162]{1,0:T(8,128)}) custom-call(bf16[45,40,96]{2,1,0:T(8,128)(2,1)} %lat_ref.1, bf16[2,45,40,96]{3,2,1,0:T(8,128)(2,1)} %cache_ref.1, f32[1,96]{1,0:T(1,128)} %bitcast.2, f32[1,96]{1,0:T(1,128)} %bitcast.3, bf16[6,162]{1,0:T(8,128)(2,1)} %w_ref.1, ...), custom_call_target="tpu_custom_call" | custom-call | tf_op jit(solution)/shard_map/pallas_call | solution.py:347
  42.5 0.0 copy-start
  42.5 1.9 %copy.12 = bf16[45,40,96]{2,1,0:T(8,128)(2,1)} copy(bf16[45,40,96]{2,1,0:T(8,128)(2,1)} %get-tuple-element.6) | data formatting | bytes 691200
  44.4 0.0 copy-done
  44.4 0.0 copy-start.1
  44.4 0.8 %copy.13 = bf16[45,40,96]{2,1,0:T(8,128)(2,1)} copy(bf16[45,40,96]{2,1,0:T(8,128)(2,1)S(1)} %copy-done) | data formatting | bytes 691200
  45.2 0.0 copy-done.1
  45.2 0.6 %copy.14 = f32[6,162]{1,0:T(8,128)} copy(f32[6,162]{1,0:T(8,128)S(1)} %copy-done.1) | data formatting | bytes 7776
Async XLA Ops:
  42.5 1.9 %copy-start = (bf16[45,40,96]{2,1,0:T(8,128)(2,1)S(1)}, bf16[45,40,96]{2,1,0:T(8,128)(2,1)}, u32[]{:S(2)}) copy-start(bf16[45,40,96]{2,1,0:T(8,128)(2,1)} %get-tuple-element.7) | copy-start | bytes 1036804
  44.4 0.8 %copy-start.1 = (f32[6,162]{1,0:T(8,128)S(1)}, f32[6,162]{1,0:T(8,128)}, u32[]{:S(2)}) copy-start(f32[6,162]{1,0:T(8,128)} %get-tuple-element.8) | copy-start | bytes 11668

commit v4 on v3

--- a/solution.py
+++ b/solution.py
@@ -65,7 +65,7 @@
     Rs, RC, SB, RA, T, PZ, RZ,
     row_s, row_r, col_s, col_r, corn_s, corn_r,
     wp_s, wp_r, wg_s, wg_r, wc_s, wc_r,
-    rc_s, rc_r, ra_s, ra_r, rz_s, rz_r,
+    rc_s, rc_r, ra_s, ra_r, rz_s, rz_r, obuf, gbuf, res_s,
 ):
     a = lax.axis_index("ha")
     b = lax.axis_index("wa")
@@ -254,6 +254,13 @@
         if t == 2:
             Wb[r, (2 - c) * 128 : (3 - c) * 128] = block
 
+    def results(h0):
+        rows = pl.ds(h0, ROWS)
+        return (
+            pltpu.make_async_copy(obuf.at[rows], out_ref.at[rows], res_s.at[0]),
+            pltpu.make_async_copy(gbuf.at[rows], glat_ref.at[rows], res_s.at[1]),
+        )
+
     def rows_step(i):
         h0 = i * ROWS
         at = pl.multiple_of(h0 * PITCH, 16)
@@ -262,7 +269,7 @@
         acc += nt(FS[pl.ds(at + 2 * PITCH, ROWS * PITCH)], Wn[2])
         acc = acc.reshape(ROWS, PITCH, 128)[:, 0:W, 0:C]
         lat = lat_ref[pl.ds(h0, ROWS)].astype(F32)
-        out_ref[pl.ds(h0, ROWS)] = (lat + bias_ref[...].reshape(1, 1, C) + acc).astype(BF16)
+        obuf[pl.ds(h0, ROWS)] = (lat + bias_ref[...].reshape(1, 1, C) + acc).astype(BF16)
 
         back = nn(FG[pl.ds(at + 2 * PITCH, ROWS * PITCH)], Wb[0])
         back += nn(FG[pl.ds(at + PITCH, ROWS * PITCH)], Wb[1])
@@ -275,7 +282,9 @@
         du = dact * (sig * (1.0 + n * (1.0 - sig))) * g
         inner = jnp.sum(lat * du, axis=2, keepdims=True) * (1.0 / C)
         dlat = scale * du - lat * (scale * scale * scale * inner)
-        glat_ref[pl.ds(h0, ROWS)] = (gout_ref[pl.ds(h0, ROWS)].astype(F32) + dlat).astype(BF16)
+        gbuf[pl.ds(h0, ROWS)] = (gout_ref[pl.ds(h0, ROWS)].astype(F32) + dlat).astype(BF16)
+        for copy in results(h0):
+            copy.start()
 
     pl.loop(0, EARLY)(rows_step)
 
@@ -332,6 +341,9 @@
         final += RZ[k]
     gw_ref[...] = final[0:6, 0:KB]
 
+    for i in range(H // ROWS):
+        for copy in results(i * ROWS):
+            copy.wait()
     for copy in halo + wpieces + wsends + pairs + asends:
         copy.wait_send()
     for itself, copy in zsends:
@@ -343,6 +355,7 @@
 
 def local(latent, frame_cache, norm_gain, conv_bias, conv_weight, grad_out):
     vmem = pl.BlockSpec(memory_space=pltpu.VMEM)
+    any_ = pl.BlockSpec(memory_space=pl.ANY)
     dma = pltpu.SemaphoreType.DMA
     return pl.pallas_call(
         kernel,
@@ -352,7 +365,7 @@
             jax.ShapeDtypeStruct((6, KB), F32),
         ),
         in_specs=[vmem] * 6,
-        out_specs=(vmem, vmem, vmem),
+        out_specs=(any_, any_, vmem),
         scratch_shapes=[
             pltpu.VMEM((4, SROWS, 128), F32),
             pltpu.VMEM((FLAT, 9 * 128), BF16),
@@ -381,6 +394,7 @@
             dma((2, 3)), dma((2, 3)), dma((2,)), dma((2,)), dma((4,)), dma((4,)),
             dma((15,)), dma((15,)), dma((15,)), dma((15,)), dma, dma,
             dma((3,)), dma((3,)), dma((2, 15)), dma((2, 15)), dma((8,)), dma((8,)),
+            pltpu.VMEM((H, W, C), BF16), pltpu.VMEM((H, W, C), BF16), dma((2,)),
         ],
         compiler_params=pltpu.CompilerParams(
             collective_id=0, has_side_effects=True, vmem_limit_bytes=60 * 1024 * 1024

time: 45.9 us -> 45.6 us (level)
  no operation moved by 1% of the time
where the time goes in v4:
time: 45.6 us; the launch traced here: 45.5 us
  Pallas kernels  41.6 us (91%)
  local copies, waits for them, and re-layouts  3.26 us (7%)
  between operations  0.65 us (1%)
    pallas_call x1, Pallas kernels, local(): pl.pallas_call(kernel, out_shape=(jax.ShapeDtypeStruct((H, W, C), BF16),...  41.6 us
    unnamed x7, local copies, waits for them, and re-layouts  3.26 us

profile of v4, /device:TPU:1, one launch (start us, length us, event | category | flops | bytes accessed | tf_op | source)
XLA Modules:
  0.0 45.5 jit_solution(1957235411691142726)
XLA Ops:
  0.6 41.6 %shard_map.85 = (bf16[45,40,96]{2,1,0:T(8,128)(2,1)}, bf16[45,40,96]{2,1,0:T(8,128)(2,1)}, f32[6,162]{1,0:T(8,128)}) custom-call(bf16[45,40,96]{2,1,0:T(8,128)(2,1)} %lat_ref.1, bf16[2,45,40,96]{3,2,1,0:T(8,128)(2,1)} %cache_ref.1, f32[1,96]{1,0:T(1,128)} %bitcast.2, f32[1,96]{1,0:T(1,128)} %bitcast.3, bf16[6,162]{1,0:T(8,128)(2,1)} %w_ref.1, ...), custom_call_target="tpu_custom_call" | custom-call | tf_op jit(solution)/shard_map/pallas_call | solution.py:360
  42.2 0.0 copy-start
  42.2 1.9 %copy.12 = bf16[45,40,96]{2,1,0:T(8,128)(2,1)} copy(bf16[45,40,96]{2,1,0:T(8,128)(2,1)} %get-tuple-element.6) | data formatting | bytes 691200
  44.1 0.0 copy-done
  44.1 0.0 copy-start.1
  44.1 0.8 %copy.13 = bf16[45,40,96]{2,1,0:T(8,128)(2,1)} copy(bf16[45,40,96]{2,1,0:T(8,128)(2,1)S(1)} %copy-done) | data formatting | bytes 691200
  44.9 0.0 copy-done.1
  44.9 0.6 %copy.14 = f32[6,162]{1,0:T(8,128)} copy(f32[6,162]{1,0:T(8,128)S(1)} %copy-done.1) | data formatting | bytes 7776
Async XLA Ops:
  42.2 1.9 %copy-start = (bf16[45,40,96]{2,1,0:T(8,128)(2,1)S(1)}, bf16[45,40,96]{2,1,0:T(8,128)(2,1)}, u32[]{:S(2)}) copy-start(bf16[45,40,96]{2,1,0:T(8,128)(2,1)} %get-tuple-element.7) | copy-start | bytes 1036804
  44.1 0.8 %copy-start.1 = (f32[6,162]{1,0:T(8,128)S(1)}, f32[6,162]{1,0:T(8,128)}, u32[]{:S(2)}) copy-start(f32[6,162]{1,0:T(8,128)} %get-tuple-element.8) | copy-start | bytes 11668
